TPU v7x, 32 devices: a whole 2x2x4 slice. The times are simulated.
32 devices in a mesh: dp: 2 (over x), row: 4 (over z), col: 4 (over y, core).
Axes of the slice: x: 2, y: 2, z: 4, core: 2. Of those that a mesh axis runs over, the one named last changes fastest.
Arguments:
- layer_input: bfloat16 [4096, 1024], P(('dp', 'col'), 'row'), may hold values from -40 to 40
- segment_ids: int32 [2, 2048], P('dp'), may hold values from 0 to 7, never falling along the last dimension, each value on 1 to 512 neighbouring positions
- norm1_gain: float32 [1024], P('row'), may hold values from 0.1 to 1.9
- in_weight: bfloat16 [1024, 3, 1024], P('row', None, 'col'), may hold values from -0.1875 to 0.1875
- conv_weight: float32 [3, 1024], P(None, 'col'), may hold values from -3 to 3
- out_weight: bfloat16 [1024, 1024], P('col', 'row'), may hold values from -0.1875 to 0.1875
- norm2_gain: float32 [1024], P('row'), may hold values from 0.1 to 1.9
- gate_up_weight: bfloat16 [1024, 2, 4608], P('row', None, 'col'), may hold values from -0.1875 to 0.1875
- down_weight: bfloat16 [4608, 1024], P('col', 'row'), may hold values from -0.09375 to 0.09375
- cotangent: bfloat16 [4096, 1024], P(('dp', 'col'), 'row'), may hold values from -6 to 6
Outputs:
- block_out: bfloat16 [4096, 1024], P(('dp', 'col'), 'row')
- grad_x: float32 [4096, 1024], P(('dp', 'col'), 'row')
- grad_norm1: float32 [1024], P('row')
- grad_in: float32 [1024, 3, 1024], P('row', None, 'col')
- grad_conv: float32 [3, 1024], P(None, 'col')
- grad_out: float32 [1024, 1024], P('col', 'row')
- grad_norm2: float32 [1024], P('row')
- grad_gate_up: float32 [1024, 2, 4608], P('row', None, 'col')
- grad_down: float32 [4608, 1024], P('col', 'row')
Inputs may be any that keep to these rules, and one draw needn't show every extreme that they name: `segment_ids`: within each sequence the ids never fall; each document has 1 to 512 tokens and one has exactly that many.
All inputs are finite; a program needn't handle non-finite values.
Results may differ from a plain program's by a relative error of at most 0.0092.
Values may be sent and summed in bfloat16 or wider, within the bound.
A program may use at most 128 MiB of HBM per device.

v0:
```python
import jax
import jax.numpy as jnp
from jax import lax
from jax.sharding import PartitionSpec as P

D = 1024
EPSILON = 1e-05


def passed_along(block, axis, distance):
    devices = range(lax.axis_size(axis))
    route = [(i - distance, i) for i in devices if i - distance in devices]
    return lax.ppermute(block, axis, route)


def spread_cols(local):
    return lax.all_gather(local, "col", axis=0, tiled=True)


def spread_rows(local):
    return lax.all_gather(local, "row", axis=0, tiled=True)


def summed_rows(whole_rows, weight, einsum_form, row_count):

    def term(row_start, count_rows):
        return jnp.einsum(einsum_form, whole_rows, weight, preferred_element_type=jnp.float32)

    return lax.psum_scatter(
        term(jnp.int32(0), row_count * lax.axis_size("row")), "row", scatter_dimension=0, tiled=True
    )


def summed_cols(whole_rows, weight, einsum_form, row_count):

    def term(row_start, count_rows):
        return jnp.einsum(einsum_form, whole_rows, weight, preferred_element_type=jnp.float32)

    return lax.psum_scatter(
        term(jnp.int32(0), row_count * lax.axis_size("col")), "col", scatter_dimension=0, tiled=True
    )


def norm_scale(inputs):
    squares = lax.psum(jnp.sum(inputs * inputs, axis=1), "row")
    return lax.rsqrt(squares / D + EPSILON)


def norm_back(inputs, scales, gains, grads):
    gained = gains * grads
    dots = lax.psum(jnp.sum(gained * inputs, axis=1), "row") / D
    return scales[:, None] * gained - inputs * (scales * scales * scales)[:, None] * dots[:, None]


def on_device(
    layer_input,
    segment_ids,
    norm1_gain,
    in_weight,
    conv_weight,
    out_weight,
    norm2_gain,
    gate_up_weight,
    down_weight,
    cotangent,
):
    seq_len = segment_ids.shape[1]
    row_tokens = seq_len // lax.axis_size("row")
    col_tokens = seq_len // lax.axis_size("col")
    row_feats = layer_input.shape[1]
    col_feats = conv_weight.shape[1]
    row_place = lax.axis_index("row")
    col_place = lax.axis_index("col")
    x_wide = layer_input.astype(jnp.float32)
    scale_one = norm_scale(x_wide)
    x_normed = (x_wide * scale_one[:, None] * norm1_gain).astype(jnp.bfloat16)
    normed_all = spread_cols(x_normed)
    mixed_in = summed_rows(normed_all, in_weight, "td,dkf->tkf", row_tokens)
    b_gate = mixed_in[:, 0]
    c_gate = mixed_in[:, 1]
    v_part = mixed_in[:, 2]
    gated_in = b_gate * v_part
    seg_padded = jnp.concatenate([jnp.full((2,), -1, jnp.int32), segment_ids[0]])
    seg_ext = lax.dynamic_slice_in_dim(seg_padded, row_place * row_tokens, row_tokens + 2, 0)
    seg_own = seg_ext[2:]
    mask_one = (seg_ext[1 : row_tokens + 1] == seg_own).astype(jnp.float32)[:, None]
    mask_two = (seg_ext[0:row_tokens] == seg_own).astype(jnp.float32)[:, None]
    prev_rows = passed_along(gated_in[row_tokens - 2 :], "row", 1)
    extended = jnp.concatenate([prev_rows, gated_in])
    prev_one = extended[1 : row_tokens + 1]
    prev_two = extended[0:row_tokens]
    conv_out = (
        conv_weight[0] * gated_in
        + conv_weight[1] * mask_one * prev_one
        + conv_weight[2] * mask_two * prev_two
    )
    mixer_out = (c_gate * conv_out).astype(jnp.bfloat16)
    mixer_all = spread_rows(mixer_out)
    resid = x_wide + summed_cols(mixer_all, out_weight, "tf,fd->td", col_tokens)
    scale_two = norm_scale(resid)
    h_normed = (resid * scale_two[:, None] * norm2_gain).astype(jnp.bfloat16)
    hn_all = spread_cols(h_normed)
    gate_up = summed_rows(hn_all, gate_up_weight, "td,dkf->tkf", row_tokens)
    gate_pre = gate_up[:, 0]
    up_pre = gate_up[:, 1]
    gate_sig = jax.nn.sigmoid(gate_pre)
    hidden = (gate_pre * gate_sig * up_pre).astype(jnp.bfloat16)
    hidden_all = spread_rows(hidden)
    block_out = (resid + summed_cols(hidden_all, down_weight, "tf,fd->td", col_tokens)).astype(
        jnp.bfloat16
    )
    cot_all = spread_cols(cotangent)
    grad_hidden = summed_rows(cot_all, down_weight, "td,fd->tf", row_tokens)
    grad_down = jnp.einsum("tf,td->fd", hidden_all, cot_all, preferred_element_type=jnp.float32)
    grad_gu = jnp.stack(
        [
            grad_hidden * up_pre * gate_sig * (1.0 + gate_pre * (1.0 - gate_sig)),
            grad_hidden * gate_pre * gate_sig,
        ],
        axis=1,
    ).astype(jnp.bfloat16)
    ggu_all = spread_rows(grad_gu)
    grad_hn = summed_cols(ggu_all, gate_up_weight, "tkf,dkf->td", col_tokens)
    grad_gate_up = jnp.einsum("td,tkf->dkf", hn_all, ggu_all, preferred_element_type=jnp.float32)
    norm2_part = jnp.sum(grad_hn * resid * scale_two[:, None], axis=0)
    grad_resid = cotangent.astype(jnp.float32) + norm_back(resid, scale_two, norm2_gain, grad_hn)
    resid_cast = grad_resid.astype(jnp.bfloat16)
    rcast_all = spread_cols(resid_cast)
    grad_mixer = summed_rows(rcast_all, out_weight, "td,fd->tf", row_tokens)
    grad_out = jnp.einsum("tf,td->fd", mixer_all, rcast_all, preferred_element_type=jnp.float32)
    grad_conv_out = grad_mixer * c_gate
    grad_c = grad_mixer * conv_out
    conv_part = jnp.stack(
        [
            jnp.sum(grad_conv_out * gated_in, axis=0),
            jnp.sum(grad_conv_out * mask_one * prev_one, axis=0),
            jnp.sum(grad_conv_out * mask_two * prev_two, axis=0),
        ]
    )
    later_one = conv_weight[1] * mask_one * grad_conv_out
    later_two = conv_weight[2] * mask_two * grad_conv_out
    next_rows = passed_along(jnp.stack([later_one[0:2], later_two[0:2]]), "row", -1)
    grad_gated = (
        conv_weight[0] * grad_conv_out
        + jnp.concatenate([later_one[1:], next_rows[0, 0:1]])
        + jnp.concatenate([later_two[2:], next_rows[1]])
    )
    grad_mixed = jnp.stack([grad_gated * v_part, grad_c, grad_gated * b_gate], axis=1).astype(
        jnp.bfloat16
    )
    gmix_all = spread_rows(grad_mixed)
    grad_xn = summed_cols(gmix_all, in_weight, "tkf,dkf->td", col_tokens)
    grad_in = jnp.einsum("td,tkf->dkf", normed_all, gmix_all, preferred_element_type=jnp.float32)
    norm1_part = jnp.sum(grad_xn * x_wide * scale_one[:, None], axis=0)
    grad_x = grad_resid + norm_back(x_wide, scale_one, norm1_gain, grad_xn)
    conv_padded = lax.dynamic_update_slice_in_dim(
        jnp.zeros((3, D), jnp.float32), conv_part, col_place * col_feats, 1
    )
    gain_padded = lax.dynamic_update_slice_in_dim(
        jnp.zeros((2, D), jnp.float32),
        jnp.stack([norm1_part, norm2_part]),
        row_place * row_feats,
        1,
    )
    conv_total, gain_total = lax.psum((conv_padded, gain_padded), ("row", "col"))
    conv_own = lax.dynamic_slice_in_dim(conv_total, col_place * col_feats, col_feats, 1)
    gain_own = lax.dynamic_slice_in_dim(gain_total, row_place * row_feats, row_feats, 1)
    grad_in, grad_out, grad_gate_up, grad_down, conv_own, gain_own = lax.psum(
        (grad_in, grad_out, grad_gate_up, grad_down, conv_own, gain_own), "dp"
    )
    return (
        block_out,
        grad_x,
        gain_own[0],
        grad_in,
        conv_own,
        grad_out,
        gain_own[1],
        grad_gate_up,
        grad_down,
    )


def solution(mesh):
    return jax.shard_map(
        on_device,
        mesh=mesh,
        in_specs=(
            P(("dp", "col"), "row"),
            P("dp", None),
            P("row"),
            P("row", None, "col"),
            P(None, "col"),
            P("col", "row"),
            P("row"),
            P("row", None, "col"),
            P("col", "row"),
            P(("dp", "col"), "row"),
        ),
        out_specs=(
            P(("dp", "col"), "row"),
            P(("dp", "col"), "row"),
            P("row"),
            P("row", None, "col"),
            P(None, "col"),
            P("col", "row"),
            P("row"),
            P("row", None, "col"),
            P("col", "row"),
        ),
        check_vma=False,
    )
```

profile of v0, /device:TPU:0, one launch (start us, length us, event | category | flops | bytes accessed | tf_op | source)
XLA Modules:
  0.0 1381.3 jit_solution(11055244738655063298)
XLA Ops:
  7.2 1.2 fusion.15
  8.4 13.5 psum.84
  21.9 0.6 multiply_multiply_fusion.4
  22.5 1.8 fusion.17
  24.4 15.0 %all-gather.9.cloned.1.call-done = bf16[2048,256]{1,0:T(8,128)(2,1)} async-done(((bf16[512,256]{1,0:T(8,128)(2,1)}), bf16[2048,256]{1,0:T(8,128)(2,1)}) %all-gather.9.cloned.1.call-update) | async-done | bytes 1048592 | tf_op jit(solution)/shard_map/all_gather | solution.py:17
  39.4 4.9 fusion.8
  44.4 0.6 copy-done.25
  45.2 110.1 %reduce-scatter.9.cloned.1.call-done = f32[512,3,256]{2,0,1:T(8,128)} async-done(((f32[2048,3,256]{2,0,1:T(8,128)}), f32[512,3,256]{2,0,1:T(8,128)}) %reduce-scatter.9.cloned.1.call-update) | async-done | bytes 1572880 | tf_op jit(solution)/shard_map/reduce_scatter | solution.py:29
  155.3 1.3 fusion.26
  156.6 3.4 collective-permute-start
  160.0 1.2 collective-permute-done
  161.3 2.2 multiply_convert_fusion.7
  163.5 29.4 %all-gather.11.cloned.1.call-done = bf16[2048,256]{1,0:T(8,128)(2,1)} async-done(((bf16[512,256]{1,0:T(8,128)(2,1)}), bf16[2048,256]{1,0:T(8,128)(2,1)}) %all-gather.11.cloned.1.call-update) | async-done | bytes 1048592 | tf_op jit(solution)/shard_map/all_gather | solution.py:21
  192.9 3.0 fusion.38
  196.0 0.5 all-gather.17.cloned.1.call-update
  196.6 30.1 %reduce-scatter.11.cloned.1.call-done = f32[512,256]{1,0:T(8,128)} async-done(((f32[2048,256]{1,0:T(8,128)}), f32[512,256]{1,0:T(8,128)}) %reduce-scatter.11.cloned.1.call-update) | async-done | bytes 524304 | tf_op jit(solution)/shard_map/reduce_scatter | solution.py:39
  226.7 1.2 multiply_reduce_fusion.5
  227.8 11.7 psum.85
  239.5 0.8 multiply_convert_fusion.6
  240.5 4.3 all-gather.17.cloned.1.call-done
  244.8 6.5 fusion.40
  251.3 12.2 all-gather.13.cloned.1.call-done
  263.5 11.0 fusion.4
  274.6 152.5 %reduce-scatter.17.cloned.1.call-done = f32[512,1152]{1,0:T(8,128)} async-done(((f32[2048,1152]{1,0:T(8,128)}), f32[512,1152]{1,0:T(8,128)}) %reduce-scatter.17.cloned.1.call-update) | async-done | bytes 2359312 | tf_op jit(solution)/shard_map/reduce_scatter | solution.py:29
  427.1 317.3 %reduce-scatter.13.cloned.1.call-done = f32[512,2,1152]{2,0,1:T(8,128)} async-done(((f32[2048,2,1152]{2,0,1:T(8,128)}), f32[512,2,1152]{2,0,1:T(8,128)}) %reduce-scatter.13.cloned.1.call-update) | async-done | bytes 4718608 | tf_op jit(solution)/shard_map/reduce_scatter | solution.py:29
  744.4 5.4 fusion.1
  749.8 1.6 pad_maximum_fusion
  751.5 0.5 all-gather.15.cloned.1.call-update
  752.1 167.2 %all-gather.19.cloned.1.call-done = bf16[2048,2,1152]{2,0,1:T(8,128)(2,1)} async-done(((bf16[512,2,1152]{2,0,1:T(8,128)(2,1)}), bf16[2048,2,1152]{2,0,1:T(8,128)(2,1)}) %all-gather.19.cloned.1.call-update) | async-done | bytes 9437200 | tf_op jit(solution)/shard_map/all_gather | solution.py:21
  919.3 7.7 convolution_bitcast_fusion.1
  927.0 0.2 reduce-scatter.15.cloned.1.call-start
  927.2 81.7 %all-gather.15.cloned.1.call-done = bf16[2048,1152]{1,0:T(8,128)(2,1)} async-done(((bf16[512,1152]{1,0:T(8,128)(2,1)}), bf16[2048,1152]{1,0:T(8,128)(2,1)}) %all-gather.15.cloned.1.call-update) | async-done | bytes 4718608 | tf_op jit(solution)/shard_map/all_gather | solution.py:21
  1008.9 5.2 fusion.39
  1014.2 27.4 %reduce-scatter.19.cloned.1.call-done = f32[512,256]{1,0:T(8,128)} async-done(((f32[2048,256]{1,0:T(8,128)}), f32[512,256]{1,0:T(8,128)}) %reduce-scatter.19.cloned.1.call-update) | async-done | bytes 524304 | tf_op jit(solution)/shard_map/reduce_scatter | solution.py:39
  1041.6 1.8 multiply_reduce_fusion.3
  1043.5 11.7 psum.86
  1055.1 20.1 %reduce-scatter.15.cloned.1.call-done = f32[512,256]{1,0:T(8,128)} async-done(((f32[2048,256]{1,0:T(8,128)}), f32[512,256]{1,0:T(8,128)}) %reduce-scatter.15.cloned.1.call-update) | async-done | bytes 524304 | tf_op jit(solution)/shard_map/reduce_scatter | solution.py:39
  1075.2 2.4 fusion.34
  1077.8 16.8 %all-gather.21.cloned.1.call-done = bf16[2048,256]{1,0:T(8,128)(2,1)} async-done(((bf16[512,256]{1,0:T(8,128)(2,1)}), bf16[2048,256]{1,0:T(8,128)(2,1)}) %all-gather.21.cloned.1.call-update) | async-done | bytes 1048592 | tf_op jit(solution)/shard_map/all_gather | solution.py:17
  1094.6 3.0 fusion.41
  1097.6 43.7 %reduce-scatter.21.cloned.1.call-done = f32[512,256]{1,0:T(8,128)} async-done(((f32[2048,256]{1,0:T(8,128)}), f32[512,256]{1,0:T(8,128)}) %reduce-scatter.21.cloned.1.call-update) | async-done | bytes 524304 | tf_op jit(solution)/shard_map/reduce_scatter | solution.py:29
  1141.4 1.4 multiply_reduce_fusion.1
  1142.8 0.2 multiply_multiply_fusion.2
  1143.0 1.3 collective-permute-start.1
  1144.4 4.1 collective-permute-done.1
  1148.8 1.0 pad_maximum_fusion.1
  1149.8 62.7 %all-gather.23.cloned.1.call-done = bf16[2048,3,256]{2,0,1:T(8,128)(2,1)} async-done(((bf16[512,3,256]{2,0,1:T(8,128)(2,1)}), bf16[2048,3,256]{2,0,1:T(8,128)(2,1)}) %all-gather.23.cloned.1.call-update) | async-done | bytes 3145744 | tf_op jit(solution)/shard_map/all_gather | solution.py:21
  1212.6 4.3 convolution_bitcast_fusion
  1217.0 4.9 fusion.43
  1221.8 8.5 fusion.2
  1230.4 1.2 fusion.42
  1231.6 1.9 fusion.6
  1233.6 13.3 reduce-scatter.23.cloned.1.call-done
  1246.9 1.3 fusion.23
  1248.2 11.7 psum.87
  1259.9 57.6 %all-reduce.1 = (f32[2,1024]{1,0:T(2,128)S(1)}, f32[3,1024]{1,0:T(4,128)S(1)}) all-reduce(f32[2,1024]{1,0:T(2,128)S(1)} %maximum_dynamic-update-slice_fusion.1, f32[3,1024]{1,0:T(4,128)S(1)} %maximum_dynamic-update-slice_fusion), channel_id=1, replica_groups=mesh['dp'=2,'row'=4,'col'=4] {'row','col'}, use_global_device_ids=true, to_apply=%region_18.0 | all-reduce | flops 5120 | bytes 40960 | tf_op jit(solution)/shard_map/psum | solution.py:165
  1317.5 5.9 all-reduce.2
  1323.4 0.6 fusion.37
  1324.0 2.1 fusion.20
  1326.1 41.0 %all-reduce.6.cloned.1.call-done = (f32[256,3,256]{2,0,1:T(8,128)}, f32[256,256]{1,0:T(8,128)}, f32[256,2,1152]{2,0,1:T(8,128)}, f32[1152,256]{1,0:T(8,128)}) async-done(((f32[256,3,256]{2,0,1:T(8,128)}, f32[256,256]{1,0:T(8,128)}, f32[256,2,1152]{2,0,1:T(8,128)}, f32[1152,256]{1,0:T(8,128)}), (f32[256,3,256]{2,0,1:T(8,128)}, f32[256,256]{1,0:T(8,128)}, f32[256,2,1152]{2,0,1:T(8,128)}, ...) | async-done | bytes 4587536 | tf_op jit(solution)/shard_map/psum | solution.py:168
  1367.1 5.0 copy.23
  1372.2 0.9 copy.38
  1373.1 0.7 copy.39
  1373.8 1.0 copy.40
  (111 shorter events, 1.6 us)
Async XLA Ops:
  7.2 256.3 %copy-start = (bf16[256,2,1152]{2,1,0:T(2,128)(2,1)S(1)}, bf16[256,2,1152]{2,1,0:T(2,128)(2,1)}, u32[]{:S(2)}) copy-start(bf16[256,2,1152]{2,1,0:T(2,128)(2,1)} %param.17) | copy-start | bytes 3538948
  7.2 32.2 %all-gather.9.cloned.1.call-start = ((), (), s32[]{:S(2)}) async-start(), calls=%async_computation.8 | async-start | bytes 1310720 | tf_op jit(solution)/shard_map/all_gather | solution.py:17
  24.3 131.0 %reduce-scatter.9.cloned.1.call-start = ((), (), s32[]{:S(2)}) async-start(), calls=%async_computation.9 | async-start | bytes 7864320 | tf_op jit(solution)/shard_map/reduce_scatter | solution.py:29
  44.3 0.7 copy-start.25
  44.3 115.6 %copy-start.29 = (f32[3,256]{1,0:T(4,128)S(1)}, f32[3,256]{1,0:T(4,128)}, u32[]{:S(2)}) copy-start(f32[3,256]{1,0:T(4,128)} %param.14) | copy-start | bytes 9220
  44.4 148.6 %copy-start.16 = (bf16[256,256]{1,0:T(8,128)(2,1)S(1)}, bf16[256,256]{1,0:T(8,128)(2,1)}, u32[]{:S(2)}) copy-start(bf16[256,256]{1,0:T(8,128)(2,1)} %param.15) | copy-start | bytes 393220
  44.4 148.6 %all-gather.11.cloned.1.call-start = ((), (), s32[]{:S(2)}) async-start(), calls=%async_computation.10 | async-start | bytes 1310720 | tf_op jit(solution)/shard_map/all_gather | solution.py:21
  156.6 4.7 collective-permute-start
  160.0 3.4 copy-start.20
  160.0 3.4 copy-start.22
  161.3 2.2 copy-start.26
  163.5 63.2 %copy-start.3 = (bf16[512,256]{1,0:T(8,128)(2,1)S(1)}, bf16[512,256]{1,0:T(8,128)(2,1)}, u32[]{:S(2)}) copy-start(bf16[512,256]{1,0:T(8,128)(2,1)} %param.10) | copy-start | bytes 786436
  163.5 63.2 %reduce-scatter.11.cloned.1.call-start = ((), (), s32[]{:S(2)}) async-start(), calls=%async_computation.11 | async-start | bytes 2621440 | tf_op jit(solution)/shard_map/reduce_scatter | solution.py:39
  195.9 43.6 %copy-start.24 = (f32[256]{0:T(256)S(1)}, f32[256]{0:T(256)}, u32[]{:S(2)}) copy-start(f32[256]{0:T(256)} %param.16) | copy-start | bytes 3076
  195.9 48.9 %copy-start.15 = (bf16[1152,256]{1,0:T(8,128)(2,1)S(1)}, bf16[1152,256]{1,0:T(8,128)(2,1)}, u32[]{:S(2)}) copy-start(bf16[1152,256]{1,0:T(8,128)(2,1)} %param.18) | copy-start | bytes 1769476
  195.9 48.9 %all-gather.17.cloned.1.call-start = ((), (), s32[]{:S(2)}) async-start(), calls=%async_computation.16 | async-start | bytes 1310720 | tf_op jit(solution)/shard_map/all_gather | solution.py:17
  196.5 67.0 %all-gather.13.cloned.1.call-start = ((), (), s32[]{:S(2)}) async-start(), calls=%async_computation.12 | async-start | bytes 1310720 | tf_op jit(solution)/shard_map/all_gather | solution.py:17
  240.4 186.7 %reduce-scatter.17.cloned.1.call-start = ((), (), s32[]{:S(2)}) async-start(), calls=%async_computation.17 | async-start | bytes 11796480 | tf_op jit(solution)/shard_map/reduce_scatter | solution.py:29
  251.3 493.1 %reduce-scatter.13.cloned.1.call-start = ((), (), s32[]{:S(2)}) async-start(), calls=%async_computation.13 | async-start | bytes 23592960 | tf_op jit(solution)/shard_map/reduce_scatter | solution.py:29
  274.5 644.8 %all-gather.19.cloned.1.call-start = ((), (), s32[]{:S(2)}) async-start(), calls=%async_computation.18 | async-start | bytes 11796480 | tf_op jit(solution)/shard_map/all_gather | solution.py:21
  751.4 257.5 %all-gather.15.cloned.1.call-start = ((), (), s32[]{:S(2)}) async-start(), calls=%async_computation.14 | async-start | bytes 5898240 | tf_op jit(solution)/shard_map/all_gather | solution.py:21
  752.0 289.6 %reduce-scatter.19.cloned.1.call-start = ((), (), s32[]{:S(2)}) async-start(), calls=%async_computation.19 | async-start | bytes 2621440 | tf_op jit(solution)/shard_map/reduce_scatter | solution.py:39
  927.0 148.2 %reduce-scatter.15.cloned.1.call-start = ((), (), s32[]{:S(2)}) async-start(), calls=%async_computation.15 | async-start | bytes 2621440 | tf_op jit(solution)/shard_map/reduce_scatter | solution.py:39
  1014.1 61.1 %copy-start.13 = (bf16[512,256]{1,0:T(8,128)(2,1)S(1)}, bf16[512,256]{1,0:T(8,128)(2,1)}, u32[]{:S(2)}) copy-start(bf16[512,256]{1,0:T(8,128)(2,1)} %param.19) | copy-start | bytes 786436
  1014.1 80.4 %copy-start.17 = (bf16[256,256]{1,0:T(8,128)(2,1)S(1)}, bf16[256,256]{1,0:T(8,128)(2,1)}, u32[]{:S(2)}) copy-start(bf16[256,256]{1,0:T(8,128)(2,1)} %param.15) | copy-start | bytes 393220
  1014.1 80.4 %all-gather.21.cloned.1.call-start = ((), (), s32[]{:S(2)}) async-start(), calls=%async_computation.20 | async-start | bytes 1310720 | tf_op jit(solution)/shard_map/all_gather | solution.py:17
  1077.7 63.7 %copy-start.4 = (f32[512,3,256]{2,0,1:T(8,128)S(1)}, f32[512,3,256]{2,0,1:T(8,128)}, u32[]{:S(2)}) copy-start(f32[512,3,256]{2,0,1:T(8,128)} %reduce-scatter.9.cloned.1.call-done) | copy-start | bytes 4718596
  1077.7 63.7 %copy-start.9 = (f32[512,256]{1,0:T(8,128)S(1)}, f32[512,256]{1,0:T(8,128)}, u32[]{:S(2)}) copy-start(f32[512,256]{1,0:T(8,128)} %get-tuple-element.41) | copy-start | bytes 1572868
  1077.7 63.7 %reduce-scatter.21.cloned.1.call-start = ((), (), s32[]{:S(2)}) async-start(), calls=%async_computation.21 | async-start | bytes 2621440 | tf_op jit(solution)/shard_map/reduce_scatter | solution.py:29
  1097.6 45.2 %copy-start.21 = (f32[1,256]{1,0:T(1,128)S(1)}, f32[1,256]{1,0:T(1,128)}, u32[]{:S(2)}) copy-start(f32[1,256]{1,0:T(1,128)} %copy-done.20) | copy-start | bytes 3076
  1097.6 45.2 %copy-start.23 = (f32[1,256]{1,0:T(1,128)S(1)}, f32[1,256]{1,0:T(1,128)}, u32[]{:S(2)}) copy-start(f32[1,256]{1,0:T(1,128)} %copy-done.22) | copy-start | bytes 3076
  1097.6 115.0 %all-gather.23.cloned.1.call-start = ((), (), s32[]{:S(2)}) async-start(), calls=%async_computation.22 | async-start | bytes 3932160 | tf_op jit(solution)/shard_map/all_gather | solution.py:21
  1143.0 5.5 collective-permute-start.1
  1149.7 67.2 %copy-start.11 = (bf16[2048,256]{1,0:T(8,128)(2,1)S(1)}, bf16[2048,256]{1,0:T(8,128)(2,1)}, u32[]{:S(2)}) copy-start(bf16[2048,256]{1,0:T(8,128)(2,1)} %all-gather.17.cloned.1.call-done) | copy-start | bytes 3145732
  1149.8 97.1 %reduce-scatter.23.cloned.1.call-start = ((), (), s32[]{:S(2)}) async-start(), calls=%async_computation.23 | async-start | bytes 2621440 | tf_op jit(solution)/shard_map/reduce_scatter | solution.py:39
  1216.9 4.9 copy-start.2
  1216.9 150.2 %all-reduce.6.cloned.1.call-start = ((), (), s32[]{:S(2)}) async-start(), calls=%async_computation.24 | async-start | bytes 9175040 | tf_op jit(solution)/shard_map/psum | solution.py:168
  1221.8 8.5 copy-start.5
  1221.8 8.5 copy-start.6
  1221.8 9.7 copy-start.8
  1230.4 1.2 copy-start.7
  1233.5 13.4 copy-start.19
  1233.5 26.4 %copy-start.28 = (f32[256]{0:T(256)S(1)}, f32[256]{0:T(256)}, u32[]{:S(2)}) copy-start(f32[256]{0:T(256)} %get-tuple-element.21) | copy-start | bytes 3076
  1233.5 90.5 %copy-start.10 = (f32[512,256]{1,0:T(8,128)S(1)}, f32[512,256]{1,0:T(8,128)}, u32[]{:S(2)}) copy-start(f32[512,256]{1,0:T(8,128)} %get-tuple-element.37) | copy-start | bytes 1572868
  1233.5 90.5 %copy-start.27 = (f32[512]{0:T(512)S(1)}, f32[512]{0:T(512)}, u32[]{:S(2)}) copy-start(f32[512]{0:T(512)} %get-tuple-element.56) | copy-start | bytes 6148
  1367.1 5.1 copy-start.14
  1367.1 5.9 copy-start.18
  1367.1 6.6 copy-start.12
  1367.1 7.6 copy-start.1
Sparse Core Ops, SparseCore 0:
  24.5 14.8 all-gather.8
  44.5 110.7 reduce-scatter.8
  163.6 29.2 all-gather.10
  196.1 30.5 reduce-scatter.10
  228.1 16.6 all-gather.16
  246.8 16.6 all-gather.12
  265.9 161.1 reduce-scatter.16
  429.4 314.8 reduce-scatter.12
  751.5 167.7 all-gather.18
  921.3 87.5 all-gather.14
  1012.0 29.5 reduce-scatter.18
  1044.0 31.1 reduce-scatter.14
  1077.8 16.7 all-gather.20
  1097.7 43.6 reduce-scatter.20
  1149.9 62.6 all-gather.22
  1217.0 29.8 reduce-scatter.22
  1250.5 116.5 all-reduce.5
where the time goes:
time: 1380 us
  waiting for transfers between devices  1150 us (83%)
  blocking collectives  112 us (8%)
  matrix products  62 us (4%)
  other arithmetic  26.7 us (2%)
  between operations  14.3 us (1%)
    reduce_scatter x4, waiting for transfers between devices, summed_rows(): lax.psum_scatter(term(jnp.int32(0), row_count * lax.axis_size('row')), 'r...  624 us
    all_gather x4, waiting for transfers between devices, spread_rows(): return lax.all_gather(local, 'row', axis=0, tiled=True)  341 us
    reduce_scatter x4, waiting for transfers between devices, summed_cols(): lax.psum_scatter(term(jnp.int32(0), row_count * lax.axis_size('col')), 'c...  90.9 us
    psum x1, blocking collectives, on_device(): lax.psum((conv_padded, gain_padded), ('row', 'col'))  57.6 us
    all_gather x4, waiting for transfers between devices, spread_cols(): return lax.all_gather(local, 'col', axis=0, tiled=True)  48.3 us
    dot_general x8, matrix products, term(): jnp.einsum(einsum_form, whole_rows, weight, preferred_element_type=jnp.fl...  45.5 us
    psum x1, waiting for transfers between devices, on_device(): lax.psum((grad_in, grad_out, grad_gate_up, grad_down, conv_own, gain_own)...  41 us
  transfers between devices with their start and end apart: 19, of which 19 were waited for; matrix products, arithmetic and copies ran while one was open for 4% of the time, Pallas kernels for 0%

commit v1 on v0

--- a/solution.py
+++ b/solution.py
@@ -7,6 +7,24 @@
 EPSILON = 1e-05
 
 
+def collect(array, axis, dim):
+    ways, here, turn = (lax.axis_size(axis), lax.axis_index(axis), array.shape[dim])
+    lengths = [n * ways if d == dim else n for d, n in enumerate(array.shape)]
+    full = lax.dynamic_update_slice_in_dim(
+        jnp.zeros(lengths, array.dtype), array, here * turn, axis=dim
+    )
+    going_up = going_down = array
+    for far in range(1, ways // 2 + 1):
+        going_up = lax.ppermute(going_up, axis, [(d, (d + 1) % ways) for d in range(ways)])
+        full = lax.dynamic_update_slice_in_dim(full, going_up, (here - far) % ways * turn, axis=dim)
+        if 2 * far < ways:
+            going_down = lax.ppermute(going_down, axis, [(d, (d - 1) % ways) for d in range(ways)])
+            full = lax.dynamic_update_slice_in_dim(
+                full, going_down, (here + far) % ways * turn, axis=dim
+            )
+    return full
+
+
 def passed_along(block, axis, distance):
     devices = range(lax.axis_size(axis))
     route = [(i - distance, i) for i in devices if i - distance in devices]
@@ -18,7 +36,7 @@
 
 
 def spread_rows(local):
-    return lax.all_gather(local, "row", axis=0, tiled=True)
+    return collect(local, "row", 0)
 
 
 def summed_rows(whole_rows, weight, einsum_form, row_count):

time: 1380 us -> 1320 us (0.957)
  waiting for transfers between devices: 1150 us -> 987 us
  starting transfers between devices: 5.56 us -> 105 us
    all_gather x4 -> x0, waiting for transfers between devices: 341 us -> none  [spread_rows(): return lax.all_gather(local, 'row', axis=0, tiled=True)]
    ppermute x0 -> x12, waiting for transfers between devices: none -> 209 us  [the longest x8 202 us: collect(): lax.ppermute(going_up, axis, [(d, (d + 1) % ways) for d in range(ways)])]
    ppermute x0 -> x12, starting transfers between devices: none -> 99.1 us  [the longest x8 86.9 us: collect(): lax.ppermute(going_up, axis, [(d, (d + 1) % ways) for d in range(ways)])]
    reduce_scatter x4, waiting for transfers between devices: 90.9 us -> 61.8 us  [summed_cols(): lax.psum_scatter(term(jnp.int32(0), row_count * lax.axis_size('col')), 'c...]
  transfers between devices with their start and end apart: 19 -> 27, of which waited for: 19 -> 25; matrix products, arithmetic and copies ran while one was open for 4% -> 4% of each run, Pallas kernels for 0% -> 0%
where the time goes in v1:
time: 1320 us
  waiting for transfers between devices  987 us (75%)
  blocking collectives  109 us (8%)
  starting transfers between devices  105 us (8%)
  matrix products  52.8 us (4%)
  other arithmetic  29.1 us (2%)
  local copies, waits for them, and re-layouts  22.3 us (2%)
  between operations  14.4 us (1%)
    reduce_scatter x4, waiting for transfers between devices, summed_rows(): lax.psum_scatter(term(jnp.int32(0), row_count * lax.axis_size('row')), 'r...  624 us
    ppermute x8, waiting for transfers between devices, collect(): lax.ppermute(going_up, axis, [(d, (d + 1) % ways) for d in range(ways)])  202 us
    ppermute x8, starting transfers between devices, collect(): lax.ppermute(going_up, axis, [(d, (d + 1) % ways) for d in range(ways)])  86.9 us
    reduce_scatter x4, waiting for transfers between devices, summed_cols(): lax.psum_scatter(term(jnp.int32(0), row_count * lax.axis_size('col')), 'c...  61.8 us
    psum x1, blocking collectives, on_device(): lax.psum((conv_padded, gain_padded), ('row', 'col'))  57.6 us
    all_gather x4, waiting for transfers between devices, spread_cols(): return lax.all_gather(local, 'col', axis=0, tiled=True)  45.7 us
    psum x1, waiting for transfers between devices, on_device(): lax.psum((grad_in, grad_out, grad_gate_up, grad_down, conv_own, gain_own)...  41.2 us
    dot_general x8, matrix products, term(): jnp.einsum(einsum_form, whole_rows, weight, preferred_element_type=jnp.fl...  36.6 us
  transfers between devices with their start and end apart: 27, of which 25 were waited for; matrix products, arithmetic and copies ran while one was open for 4% of the time, Pallas kernels for 0%

profile of v1, /device:TPU:0, one launch (start us, length us, event | category | flops | bytes accessed | tf_op | source)
XLA Modules:
  0.0 1319.3 jit_solution(18166730228772591350)
XLA Ops:
  8.4 13.5 %psum.84 = f32[512]{0:T(512)S(1)} all-reduce(f32[512]{0:T(512)S(1)} %fusion.15), channel_id=1, replica_groups=mesh['dp'=2,'row'=4,'col'=4] {'row'}, use_global_device_ids=true, to_apply=%region_1.0 | all-reduce | flops 512 | bytes 4096 | tf_op jit(solution)/shard_map/psum | solution.py:63
  22.5 1.8 fusion.17
  24.4 15.0 %all-gather.5.cloned.1.call-done = bf16[2048,256]{1,0:T(8,128)(2,1)} async-done(((bf16[512,256]{1,0:T(8,128)(2,1)}), bf16[2048,256]{1,0:T(8,128)(2,1)}) %all-gather.5.cloned.1.call-update) | async-done | bytes 1048592 | tf_op jit(solution)/shard_map/all_gather | solution.py:35
  39.4 5.0 fusion.8
  45.2 110.1 %reduce-scatter.9.cloned.1.call-done = f32[512,3,256]{2,0,1:T(8,128)} async-done(((f32[2048,3,256]{2,0,1:T(8,128)}), f32[512,3,256]{2,0,1:T(8,128)}) %reduce-scatter.9.cloned.1.call-update) | async-done | bytes 1572880 | tf_op jit(solution)/shard_map/reduce_scatter | solution.py:47
  156.6 3.4 collective-permute-start
  161.4 2.1 constant_dynamic-update-slice_fusion.17
  163.5 2.3 collective-permute-start.1
  165.8 1.5 collective-permute-start.2
  167.3 7.2 collective-permute-done.1
  174.5 2.9 collective-permute-start.3
  177.5 2.7 collective-permute-done.2
  181.1 2.7 collective-permute-done.3
  184.8 1.8 fusion.38
  187.2 30.8 %reduce-scatter.11.cloned.1.call-done = f32[512,256]{1,0:T(8,128)} async-done(((f32[2048,256]{1,0:T(8,128)}), f32[512,256]{1,0:T(8,128)}) %reduce-scatter.11.cloned.1.call-update) | async-done | bytes 524304 | tf_op jit(solution)/shard_map/reduce_scatter | solution.py:57
  219.2 12.3 psum.85
  232.7 1.5 multiply_convert_fusion.6
  234.3 1.8 all-gather.9.cloned.1.call-done
  236.2 6.6 fusion.40
  242.8 12.1 all-gather.7.cloned.1.call-done
  254.9 11.0 fusion.4
  265.9 152.4 %reduce-scatter.17.cloned.1.call-done = f32[512,1152]{1,0:T(8,128)} async-done(((f32[2048,1152]{1,0:T(8,128)}), f32[512,1152]{1,0:T(8,128)}) %reduce-scatter.17.cloned.1.call-update) | async-done | bytes 2359312 | tf_op jit(solution)/shard_map/reduce_scatter | solution.py:47
  418.3 317.3 %reduce-scatter.13.cloned.1.call-done = f32[512,2,1152]{2,0,1:T(8,128)} async-done(((f32[2048,2,1152]{2,0,1:T(8,128)}), f32[512,2,1152]{2,0,1:T(8,128)}) %reduce-scatter.13.cloned.1.call-update) | async-done | bytes 4718608 | tf_op jit(solution)/shard_map/reduce_scatter | solution.py:47
  735.6 4.2 fusion.1
  741.2 3.7 collective-permute-start.8
  744.8 52.1 %collective-permute-done.7 = bf16[512,2,1152]{2,0,1:T(8,128)(2,1)S(1)} collective-permute-done((bf16[512,2,1152]{2,0,1:T(8,128)(2,1)S(1)}, bf16[512,2,1152]{2,0,1:T(8,128)(2,1)S(1)}, u32[]{:S(2)}, u32[]{:S(2)}) %collective-permute-start.7) | collective-permute-done | bytes 2359328 | tf_op jit(solution)/shard_map/ppermute | solution.py:18
  797.0 49.0 %collective-permute-start.9 = (bf16[512,2,1152]{2,0,1:T(8,128)(2,1)S(1)}, bf16[512,2,1152]{2,0,1:T(8,128)(2,1)S(1)}, u32[]{:S(2)}, u32[]{:S(2)}) collective-permute-start(bf16[512,2,1152]{2,0,1:T(8,128)(2,1)S(1)} %collective-permute-done.7), channel_id=1, source_target_pairs={{0,4},{4,8},{8,12},{12,0},{1,5},{5,9},{9,13},{13,1},{2,6},{6,10},{... | collective-permute-start | bytes 7077896 | tf_op jit(solution)/shard_map/ppermute | solution.py:18
  846.7 51.5 %collective-permute-done.9 = bf16[512,2,1152]{2,0,1:T(8,128)(2,1)S(1)} collective-permute-done((bf16[512,2,1152]{2,0,1:T(8,128)(2,1)S(1)}, bf16[512,2,1152]{2,0,1:T(8,128)(2,1)S(1)}, u32[]{:S(2)}, u32[]{:S(2)}) %collective-permute-start.9) | collective-permute-done | bytes 2359328 | tf_op jit(solution)/shard_map/ppermute | solution.py:18
  898.6 3.6 copy-done.2
  902.2 4.1 convolution_bitcast_fusion.1
  906.8 3.1 constant_dynamic-update-slice_fusion.13
  909.9 3.8 collective-permute-start.5
  913.7 26.8 %collective-permute-done.4 = bf16[512,1152]{1,0:T(8,128)(2,1)S(1)} collective-permute-done((bf16[512,1152]{1,0:T(8,128)(2,1)S(1)}, bf16[512,1152]{1,0:T(8,128)(2,1)S(1)}, u32[]{:S(2)}, u32[]{:S(2)}) %collective-permute-start.4) | collective-permute-done | bytes 1179680 | tf_op jit(solution)/shard_map/ppermute | solution.py:18
  940.6 20.1 %collective-permute-start.6 = (bf16[512,1152]{1,0:T(8,128)(2,1)S(1)}, bf16[512,1152]{1,0:T(8,128)(2,1)S(1)}, u32[]{:S(2)}, u32[]{:S(2)}) collective-permute-start(bf16[512,1152]{1,0:T(8,128)(2,1)S(1)} %collective-permute-done.4), channel_id=1, source_target_pairs={{0,4},{4,8},{8,12},{12,0},{1,5},{5,9},{9,13},{13,1},{2,6},{6,10},{... | collective-permute-start | bytes 3538952 | tf_op jit(solution)/shard_map/ppermute | solution.py:18
  960.8 1.5 collective-permute-done.5
  962.5 26.2 %collective-permute-done.6 = bf16[512,1152]{1,0:T(8,128)(2,1)S(1)} collective-permute-done((bf16[512,1152]{1,0:T(8,128)(2,1)S(1)}, bf16[512,1152]{1,0:T(8,128)(2,1)S(1)}, u32[]{:S(2)}, u32[]{:S(2)}) %collective-permute-start.6) | collective-permute-done | bytes 1179680 | tf_op jit(solution)/shard_map/ppermute | solution.py:18
  988.9 2.2 copy-done.8
  991.1 2.8 fusion.39
  994.1 1.9 multiply_reduce_fusion.3
  995.9 8.3 psum.86
  1004.3 18.8 %reduce-scatter.15.cloned.1.call-done = f32[512,256]{1,0:T(8,128)} async-done(((f32[2048,256]{1,0:T(8,128)}), f32[512,256]{1,0:T(8,128)}) %reduce-scatter.15.cloned.1.call-update) | async-done | bytes 524304 | tf_op jit(solution)/shard_map/reduce_scatter | solution.py:57
  1023.1 2.4 fusion.34
  1025.7 16.8 %all-gather.11.cloned.1.call-done = bf16[2048,256]{1,0:T(8,128)(2,1)} async-done(((bf16[512,256]{1,0:T(8,128)(2,1)}), bf16[2048,256]{1,0:T(8,128)(2,1)}) %all-gather.11.cloned.1.call-update) | async-done | bytes 1048592 | tf_op jit(solution)/shard_map/all_gather | solution.py:35
  1042.4 3.0 fusion.41
  1045.5 43.7 %reduce-scatter.21.cloned.1.call-done = f32[512,256]{1,0:T(8,128)} async-done(((f32[2048,256]{1,0:T(8,128)}), f32[512,256]{1,0:T(8,128)}) %reduce-scatter.21.cloned.1.call-update) | async-done | bytes 524304 | tf_op jit(solution)/shard_map/reduce_scatter | solution.py:47
  1089.3 2.1 multiply_reduce_fusion.1
  1093.1 4.1 collective-permute-done.10
  1098.5 3.2 collective-permute-start.12
  1101.7 18.4 %collective-permute-done.11 = bf16[512,3,256]{2,0,1:T(8,128)(2,1)S(1)} collective-permute-done((bf16[512,3,256]{2,0,1:T(8,128)(2,1)S(1)}, bf16[512,3,256]{2,0,1:T(8,128)(2,1)S(1)}, u32[]{:S(2)}, u32[]{:S(2)}) %collective-permute-start.11) | collective-permute-done | bytes 786464 | tf_op jit(solution)/shard_map/ppermute | solution.py:18
  1120.1 11.6 collective-permute-start.13
  1131.7 2.5 collective-permute-done.12
  1134.3 16.9 %collective-permute-done.13 = bf16[512,3,256]{2,0,1:T(8,128)(2,1)S(1)} collective-permute-done((bf16[512,3,256]{2,0,1:T(8,128)(2,1)S(1)}, bf16[512,3,256]{2,0,1:T(8,128)(2,1)S(1)}, u32[]{:S(2)}, u32[]{:S(2)}) %collective-permute-start.13) | collective-permute-done | bytes 786464 | tf_op jit(solution)/shard_map/ppermute | solution.py:18
  1151.2 1.6 copy-done.3
  1152.8 2.4 convolution_bitcast_fusion
  1155.5 4.8 fusion.43
  1160.3 8.3 fusion.2
  1169.9 1.9 fusion.6
  1172.5 12.2 reduce-scatter.23.cloned.1.call-done
  1186.0 11.7 psum.87
  1197.7 57.6 %all-reduce.1 = (f32[2,1024]{1,0:T(2,128)S(1)}, f32[3,1024]{1,0:T(4,128)S(1)}) all-reduce(f32[2,1024]{1,0:T(2,128)S(1)} %constant_dynamic-update-slice_fusion.1, f32[3,1024]{1,0:T(4,128)S(1)} %constant_dynamic-update-slice_fusion), channel_id=1, replica_groups=mesh['dp'=2,'row'=4,'col'=4] {'row','col'}, use_global_device_ids=true, to_apply=%region_18.19 | all-reduce | flops 5120 | bytes 40960 | tf_op jit(solution)/shard_map/psum | solution.py:183
  1255.4 5.9 all-reduce.2
  1261.8 2.1 fusion.20
  1263.9 41.2 %all-reduce.6.cloned.1.call-done = (f32[256,3,256]{2,0,1:T(8,128)}, f32[256,256]{1,0:T(8,128)}, f32[256,2,1152]{2,0,1:T(8,128)}, f32[1152,256]{1,0:T(8,128)}) async-done(((f32[256,3,256]{2,0,1:T(8,128)}, f32[256,256]{1,0:T(8,128)}, f32[256,2,1152]{2,0,1:T(8,128)}, f32[1152,256]{1,0:T(8,128)}), (f32[256,3,256]{2,0,1:T(8,128)}, f32[256,256]{1,0:T(8,128)}, f32[256,2,1152]{2,0,1:T(8,128)}, ...) | async-done | bytes 4587536 | tf_op jit(solution)/shard_map/psum | solution.py:186
  1305.1 5.0 copy.23
  (160 shorter events, 24.1 us)
Async XLA Ops:
  7.2 247.7 %copy-start = (bf16[256,2,1152]{2,1,0:T(2,128)(2,1)S(1)}, bf16[256,2,1152]{2,1,0:T(2,128)(2,1)}, u32[]{:S(2)}) copy-start(bf16[256,2,1152]{2,1,0:T(2,128)(2,1)} %param.17) | copy-start | bytes 3538948
  7.2 32.2 %all-gather.5.cloned.1.call-start = ((), (), s32[]{:S(2)}) async-start(), calls=%async_computation.8 | async-start | bytes 1310720 | tf_op jit(solution)/shard_map/all_gather | solution.py:35
  24.3 131.0 %reduce-scatter.9.cloned.1.call-start = ((), (), s32[]{:S(2)}) async-start(), calls=%async_computation.9 | async-start | bytes 7864320 | tf_op jit(solution)/shard_map/reduce_scatter | solution.py:47
  44.3 115.6 %copy-start.39 = (f32[3,256]{1,0:T(4,128)S(1)}, f32[3,256]{1,0:T(4,128)}, u32[]{:S(2)}) copy-start(f32[3,256]{1,0:T(4,128)} %param.14) | copy-start | bytes 9220
  44.4 173.6 %reduce-scatter.11.cloned.1.call-start = ((), (), s32[]{:S(2)}) async-start(), calls=%async_computation.10 | async-start | bytes 2621440 | tf_op jit(solution)/shard_map/reduce_scatter | solution.py:57
  156.6 4.7 collective-permute-start
  160.0 3.5 copy-start.25
  160.0 3.4 copy-start.27
  160.0 24.8 %copy-start.23 = (f32[1,256]{1,0:T(1,128)}, f32[1,256]{1,0:T(1,128)S(1)}, u32[]{:S(2)}) copy-start(f32[1,256]{1,0:T(1,128)S(1)} %get-tuple-element.55) | copy-start | bytes 3076
  161.3 2.2 copy-start.33
  161.3 23.5 %copy-start.18 = (bf16[256,256]{1,0:T(8,128)(2,1)S(1)}, bf16[256,256]{1,0:T(8,128)(2,1)}, u32[]{:S(2)}) copy-start(bf16[256,256]{1,0:T(8,128)(2,1)} %param.15) | copy-start | bytes 393220
  163.5 11.1 collective-permute-start.1
  165.8 14.4 %collective-permute-start.2 = (bf16[512,256]{1,0:T(8,128)(2,1)S(1)}, bf16[512,256]{1,0:T(8,128)(2,1)}, u32[]{:S(2)}, u32[]{:S(2)}) collective-permute-start(bf16[512,256]{1,0:T(8,128)(2,1)S(1)} %get-tuple-element.43), channel_id=1, source_target_pairs={{0,12},{4,0},{8,4},{12,8},{1,13},{5,1},{9,5},{13,9},{2,14},{6,2},{... | collective-permute-start | bytes 786440 | tf_op jit(solution)/shard_map/ppermute | solution.py:21
  174.5 9.3 collective-permute-start.3
  184.8 33.2 %copy-start.6 = (bf16[512,256]{1,0:T(8,128)(2,1)S(1)}, bf16[512,256]{1,0:T(8,128)(2,1)}, u32[]{:S(2)}) copy-start(bf16[512,256]{1,0:T(8,128)(2,1)} %param.10) | copy-start | bytes 786436
  186.6 49.5 %all-gather.9.cloned.1.call-start = ((), (), s32[]{:S(2)}) async-start(), calls=%async_computation.14 | async-start | bytes 1310720 | tf_op jit(solution)/shard_map/all_gather | solution.py:35
  187.2 67.7 %all-gather.7.cloned.1.call-start = ((), (), s32[]{:S(2)}) async-start(), calls=%async_computation.11 | async-start | bytes 1310720 | tf_op jit(solution)/shard_map/all_gather | solution.py:35
  234.3 184.0 %reduce-scatter.17.cloned.1.call-start = ((), (), s32[]{:S(2)}) async-start(), calls=%async_computation.15 | async-start | bytes 11796480 | tf_op jit(solution)/shard_map/reduce_scatter | solution.py:47
  242.8 492.8 %reduce-scatter.13.cloned.1.call-start = ((), (), s32[]{:S(2)}) async-start(), calls=%async_computation.12 | async-start | bytes 23592960 | tf_op jit(solution)/shard_map/reduce_scatter | solution.py:47
  265.9 728.2 %reduce-scatter.19.cloned.1.call-start = ((), (), s32[]{:S(2)}) async-start(), calls=%async_computation.16 | async-start | bytes 2621440 | tf_op jit(solution)/shard_map/reduce_scatter | solution.py:57
  741.0 56.0 %collective-permute-start.7 = (bf16[512,2,1152]{2,0,1:T(8,128)(2,1)S(1)}, bf16[512,2,1152]{2,0,1:T(8,128)(2,1)S(1)}, u32[]{:S(2)}, u32[]{:S(2)}) collective-permute-start(bf16[512,2,1152]{2,0,1:T(8,128)(2,1)S(1)} %get-tuple-element.47), channel_id=1, source_target_pairs={{0,4},{4,8},{8,12},{12,0},{1,5},{5,9},{9,13},{13,1},{2,6},{6,10},{... | collective-permute-start | bytes 7077896 | tf_op jit(solution)/shard_map/ppermute | solution.py:18
  741.2 105.2 %collective-permute-start.8 = (bf16[512,2,1152]{2,0,1:T(8,128)(2,1)S(1)}, bf16[512,2,1152]{2,0,1:T(8,128)(2,1)S(1)}, u32[]{:S(2)}, u32[]{:S(2)}) collective-permute-start(bf16[512,2,1152]{2,0,1:T(8,128)(2,1)S(1)} %get-tuple-element.47), channel_id=1, source_target_pairs={{0,12},{4,0},{8,4},{12,8},{1,13},{5,1},{9,5},{13,9},{2,14},{6,2},{... | collective-permute-start | bytes 7077896 | tf_op jit(solution)/shard_map/ppermute | solution.py:21
  797.0 101.3 %collective-permute-start.9 = (bf16[512,2,1152]{2,0,1:T(8,128)(2,1)S(1)}, bf16[512,2,1152]{2,0,1:T(8,128)(2,1)S(1)}, u32[]{:S(2)}, u32[]{:S(2)}) collective-permute-start(bf16[512,2,1152]{2,0,1:T(8,128)(2,1)S(1)} %collective-permute-done.7), channel_id=1, source_target_pairs={{0,4},{4,8},{8,12},{12,0},{1,5},{5,9},{9,13},{13,1},{2,6},{6,10},{... | collective-permute-start | bytes 7077896 | tf_op jit(solution)/shard_map/ppermute | solution.py:18
  898.6 3.6 copy-start.2
  906.4 116.8 %reduce-scatter.15.cloned.1.call-start = ((), (), s32[]{:S(2)}) async-start(), calls=%async_computation.13 | async-start | bytes 2621440 | tf_op jit(solution)/shard_map/reduce_scatter | solution.py:57
  909.9 30.7 %collective-permute-start.4 = (bf16[512,1152]{1,0:T(8,128)(2,1)S(1)}, bf16[512,1152]{1,0:T(8,128)(2,1)S(1)}, u32[]{:S(2)}, u32[]{:S(2)}) collective-permute-start(bf16[512,1152]{1,0:T(8,128)(2,1)S(1)} %get-tuple-element.39), channel_id=1, source_target_pairs={{0,4},{4,8},{8,12},{12,0},{1,5},{5,9},{9,13},{13,1},{2,6},{6,10},{... | collective-permute-start | bytes 3538952 | tf_op jit(solution)/shard_map/ppermute | solution.py:18
  909.9 52.4 %collective-permute-start.5 = (bf16[512,1152]{1,0:T(8,128)(2,1)S(1)}, bf16[512,1152]{1,0:T(8,128)(2,1)S(1)}, u32[]{:S(2)}, u32[]{:S(2)}) collective-permute-start(bf16[512,1152]{1,0:T(8,128)(2,1)S(1)} %get-tuple-element.39), channel_id=1, source_target_pairs={{0,12},{4,0},{8,4},{12,8},{1,13},{5,1},{9,5},{13,9},{2,14},{6,2},{... | collective-permute-start | bytes 3538952 | tf_op jit(solution)/shard_map/ppermute | solution.py:21
  940.6 48.1 %collective-permute-start.6 = (bf16[512,1152]{1,0:T(8,128)(2,1)S(1)}, bf16[512,1152]{1,0:T(8,128)(2,1)S(1)}, u32[]{:S(2)}, u32[]{:S(2)}) collective-permute-start(bf16[512,1152]{1,0:T(8,128)(2,1)S(1)} %collective-permute-done.4), channel_id=1, source_target_pairs={{0,4},{4,8},{8,12},{12,0},{1,5},{5,9},{9,13},{13,1},{2,6},{6,10},{... | collective-permute-start | bytes 3538952 | tf_op jit(solution)/shard_map/ppermute | solution.py:18
  960.8 30.3 %copy-start.17 = (bf16[1152,256]{1,0:T(8,128)(2,1)S(1)}, bf16[1152,256]{1,0:T(8,128)(2,1)}, u32[]{:S(2)}) copy-start(bf16[1152,256]{1,0:T(8,128)(2,1)} %param.18) | copy-start | bytes 1769476
  988.9 2.2 copy-start.8
  991.1 3.0 copy-start.29
  993.9 29.2 %copy-start.15 = (bf16[512,256]{1,0:T(8,128)(2,1)S(1)}, bf16[512,256]{1,0:T(8,128)(2,1)}, u32[]{:S(2)}) copy-start(bf16[512,256]{1,0:T(8,128)(2,1)} %param.19) | copy-start | bytes 786436
  993.9 29.2 %copy-start.30 = (f32[512]{0:T(512)S(1)}, f32[512]{0:T(512)}, u32[]{:S(2)}) copy-start(f32[512]{0:T(512)} %get-tuple-element.64) | copy-start | bytes 6148
  994.0 48.5 %copy-start.19 = (bf16[256,256]{1,0:T(8,128)(2,1)S(1)}, bf16[256,256]{1,0:T(8,128)(2,1)}, u32[]{:S(2)}) copy-start(bf16[256,256]{1,0:T(8,128)(2,1)} %param.15) | copy-start | bytes 393220
  994.0 48.5 %all-gather.11.cloned.1.call-start = ((), (), s32[]{:S(2)}) async-start(), calls=%async_computation.17 | async-start | bytes 1310720 | tf_op jit(solution)/shard_map/all_gather | solution.py:35
  1025.6 63.7 %copy-start.11 = (f32[512,256]{1,0:T(8,128)S(1)}, f32[512,256]{1,0:T(8,128)}, u32[]{:S(2)}) copy-start(f32[512,256]{1,0:T(8,128)} %get-tuple-element.44) | copy-start | bytes 1572868
  1025.6 63.7 %copy-start.34 = (f32[2,256]{1,0:T(2,128)S(1)}, f32[2,256]{1,0:T(2,128)}, u32[]{:S(2)}) copy-start(f32[2,256]{1,0:T(2,128)} %copy-done.33) | copy-start | bytes 6148
  1025.6 63.7 %reduce-scatter.21.cloned.1.call-start = ((), (), s32[]{:S(2)}) async-start(), calls=%async_computation.18 | async-start | bytes 2621440 | tf_op jit(solution)/shard_map/reduce_scatter | solution.py:47
  1045.5 45.9 %copy-start.26 = (f32[1,256]{1,0:T(1,128)S(1)}, f32[1,256]{1,0:T(1,128)}, u32[]{:S(2)}) copy-start(f32[1,256]{1,0:T(1,128)} %copy-done.25) | copy-start | bytes 3076
  1045.5 45.9 %copy-start.28 = (f32[1,256]{1,0:T(1,128)S(1)}, f32[1,256]{1,0:T(1,128)}, u32[]{:S(2)}) copy-start(f32[1,256]{1,0:T(1,128)} %copy-done.27) | copy-start | bytes 3076
  1045.5 139.2 %reduce-scatter.23.cloned.1.call-start = ((), (), s32[]{:S(2)}) async-start(), calls=%async_computation.19 | async-start | bytes 2621440 | tf_op jit(solution)/shard_map/reduce_scatter | solution.py:57
  1091.3 5.9 copy-start.7
  1091.4 5.9 copy-start.24
  1091.6 5.6 collective-permute-start.10
  1097.8 22.3 %collective-permute-start.11 = (bf16[512,3,256]{2,0,1:T(8,128)(2,1)S(1)}, bf16[512,3,256]{2,0,1:T(8,128)(2,1)S(1)}, u32[]{:S(2)}, u32[]{:S(2)}) collective-permute-start(bf16[512,3,256]{2,0,1:T(8,128)(2,1)S(1)} %get-tuple-element.49), channel_id=1, source_target_pairs={{0,4},{4,8},{8,12},{12,0},{1,5},{5,9},{9,13},{13,1},{2,6},{6,10},{... | collective-permute-start | bytes 2359304 | tf_op jit(solution)/shard_map/ppermute | solution.py:18
  1098.5 35.7 %collective-permute-start.12 = (bf16[512,3,256]{2,0,1:T(8,128)(2,1)S(1)}, bf16[512,3,256]{2,0,1:T(8,128)(2,1)S(1)}, u32[]{:S(2)}, u32[]{:S(2)}) collective-permute-start(bf16[512,3,256]{2,0,1:T(8,128)(2,1)S(1)} %get-tuple-element.49), channel_id=1, source_target_pairs={{0,12},{4,0},{8,4},{12,8},{1,13},{5,1},{9,5},{13,9},{2,14},{6,2},{... | collective-permute-start | bytes 2359304 | tf_op jit(solution)/shard_map/ppermute | solution.py:21
  1120.1 31.1 %collective-permute-start.13 = (bf16[512,3,256]{2,0,1:T(8,128)(2,1)S(1)}, bf16[512,3,256]{2,0,1:T(8,128)(2,1)S(1)}, u32[]{:S(2)}, u32[]{:S(2)}) collective-permute-start(bf16[512,3,256]{2,0,1:T(8,128)(2,1)S(1)} %collective-permute-done.11), channel_id=1, source_target_pairs={{0,4},{4,8},{8,12},{12,0},{1,5},{5,9},{9,13},{13,1},{2,6},{6,10},{... | collective-permute-start | bytes 2359304 | tf_op jit(solution)/shard_map/ppermute | solution.py:18
  1131.7 21.2 %copy-start.20 = (bf16[256,3,256]{2,0,1:T(8,128)(2,1)S(1)}, bf16[256,3,256]{2,0,1:T(8,128)(2,1)}, u32[]{:S(2)}) copy-start(bf16[256,3,256]{2,0,1:T(8,128)(2,1)} %param.13) | copy-start | bytes 1179652
  1151.2 1.6 copy-start.3
  1152.8 2.7 copy-start.13
  1155.2 5.1 copy-start.5
  1155.2 149.8 %all-reduce.6.cloned.1.call-start = ((), (), s32[]{:S(2)}) async-start(), calls=%async_computation.20 | async-start | bytes 9175040 | tf_op jit(solution)/shard_map/psum | solution.py:186
  1160.3 8.3 copy-start.9
  1160.3 9.5 copy-start.4
  1168.6 1.2 copy-start.10
  1171.8 0.7 copy-start.37
  1171.8 12.9 copy-start.22
  1171.8 25.9 %copy-start.38 = (f32[256]{0:T(256)S(1)}, f32[256]{0:T(256)}, u32[]{:S(2)}) copy-start(f32[256]{0:T(256)} %get-tuple-element.21) | copy-start | bytes 3076
  1171.8 90.0 %copy-start.12 = (f32[512,256]{1,0:T(8,128)S(1)}, f32[512,256]{1,0:T(8,128)}, u32[]{:S(2)}) copy-start(f32[512,256]{1,0:T(8,128)} %get-tuple-element.37) | copy-start | bytes 1572868
  1171.8 90.0 %copy-start.32 = (f32[512]{0:T(512)S(1)}, f32[512]{0:T(512)}, u32[]{:S(2)}) copy-start(f32[512]{0:T(512)} %get-tuple-element.62) | copy-start | bytes 6148
  1305.1 5.1 copy-start.16
  1305.1 5.9 copy-start.21
  1305.1 6.6 copy-start.14
  1305.1 7.6 copy-start.1
  (3 other events, 2.1 us)
Sparse Core Ops, SparseCore 0:
  24.4 14.8 all-gather.4
  44.5 110.7 reduce-scatter.8
  186.7 31.2 reduce-scatter.10
  219.4 16.6 all-gather.8
  238.1 16.6 all-gather.6
  257.1 161.1 reduce-scatter.16
  420.7 314.8 reduce-scatter.12
  906.5 30.4 reduce-scatter.18
  994.1 28.9 reduce-scatter.14
  1025.7 16.6 all-gather.10
  1045.6 43.6 reduce-scatter.20
  1155.3 29.2 reduce-scatter.22
  1188.5 116.5 all-reduce.5
